TPU v7x, 32 devices: a whole 2x2x4 slice. The times are simulated.
32 devices in a mesh: ra: 8 (over z, y), dec: 4 (over x, core).
Axes of the slice: x: 2, y: 2, z: 4, core: 2. Of those that a mesh axis runs over, the one named last changes fastest.
Arguments:
- exposures: float32 [2, 1280, 3072], P(None, 'dec', 'ra'), may hold values from -6 to 6
- inv_variance: float32 [2, 1280, 3072], P(None, 'dec', 'ra'), may hold values from 0.25 to 4
- pixel_valid: int32 [2, 1280, 3072], P(None, 'dec', 'ra'), may hold values 0 or 1
- correlation: int32 [4, 8, 2], P('dec', 'ra'), may hold values 0 or 1
- pixel_offset: int32 [4, 8, 2, 2], P('dec', 'ra'), may hold values from -3 to 3
- subpixel: float32 [4, 8, 2, 2], P('dec', 'ra'), may hold values from -0.5 to 0.5
- psf_match: bfloat16 [63, 63], replicated, may hold values from -0.09375 to 0.09375
Outputs:
- matched: float32 [768, 2048], P('dec', 'ra')
- weight_map: float32 [768, 2048], P('dec', 'ra')
All inputs are finite; a program needn't handle non-finite values. No bound on the sum of `pixel_valid` or of `correlation` on one device may be relied on, other than what follows from the above.
Results may differ from a plain program's by a relative error of at most 0.007.
Values may be sent and summed in bfloat16 or wider, within the bound.
A program may use at most 128 MiB of HBM per device.

v0:
```python
import functools

import jax
import jax.numpy as jnp
from jax import lax
from jax.experimental import pallas as pl
from jax.experimental.pallas import tpu as pltpu
from jax.sharding import PartitionSpec as P

MARGIN = 64
HALF = 31
LANES = 128
BAND = 96
GROUP = 16
F32 = jnp.float32
BF16 = jnp.bfloat16
MESH = pl.DeviceIdType.MESH


def dot(a, b):
    return jnp.dot(a, b, preferred_element_type=F32)


def dot_t(a, b):
    return lax.dot_general(a, b, (((1,), (1,)), ((), ())), preferred_element_type=F32)


def sinc(x):
    angle = jnp.pi * x
    safe = jnp.where(angle == 0.0, 1.0, angle)
    return jnp.where(angle == 0.0, 1.0, jnp.sin(safe) / safe)


def lanczos(x):
    return jnp.where(jnp.abs(x) < 3.0, sinc(x) * sinc(x / 3.0), 0.0)


def skewed(row, count, width, shift):
    spread = jnp.broadcast_to(row, (count, row.shape[1]))
    return pltpu.roll(spread, shift, 1, stride=1, stride_axis=0)[:, :width]


def halves(value):
    high = value.astype(BF16)
    return high, (value - high.astype(F32)).astype(BF16)


def signed_lanes(width):
    lane = lax.broadcasted_iota(jnp.int32, (1, width), 1)
    return jnp.where(lane >= width // 2, lane - width, lane).astype(F32)


def kernel(
    dims,
    exp_hbm,
    inv_hbm,
    val_hbm,
    cor_ref,
    off_ref,
    sub_ref,
    psf_ref,
    matched_ref,
    weight_ref,
    exp_ref,
    inv_ref,
    val_ref,
    tile,
    dec_out,
    dec_in,
    ra_out,
    ra_in,
    taps,
    bands,
    coadd,
    shifts,
    load_sem,
    dec_send,
    dec_recv,
    ra_send,
    ra_recv,
):
    epochs, prows, pcols, n_ra, n_dec = dims
    rows, cols = prows - 2 * MARGIN, pcols - 2 * MARGIN
    me_ra, me_dec = lax.axis_index("ra"), lax.axis_index("dec")
    prev_ra, next_ra = lax.rem(me_ra + n_ra - 1, n_ra), lax.rem(me_ra + 1, n_ra)
    has_prev, has_next = me_dec > 0, me_dec < n_dec - 1

    loads = []
    for e in range(epochs):
        for which, (src, dst) in enumerate(
            ((exp_hbm, exp_ref), (inv_hbm, inv_ref), (val_hbm, val_ref))
        ):
            loads.append(pltpu.make_async_copy(src.at[e], dst.at[e], load_sem.at[3 * e + which]))
    for copy in loads:
        copy.start()

    barrier = pltpu.get_barrier_semaphore()
    for peer in (prev_ra, next_ra):
        pl.semaphore_signal(barrier, inc=1, device_id=(peer, me_dec), device_id_type=MESH)

    @pl.when(has_prev)
    def _():
        pl.semaphore_signal(barrier, inc=1, device_id=(me_ra, me_dec - 1), device_id_type=MESH)

    @pl.when(has_next)
    def _():
        pl.semaphore_signal(barrier, inc=1, device_id=(me_ra, me_dec + 1), device_id_type=MESH)

    half = prows // 2
    side = 256
    start = prows - side
    maps = []
    for e in range(epochs):
        lanes = signed_lanes(512)
        shift_r = off_ref[0, 0, e, 0].astype(F32) + sub_ref[0, 0, e, 0]
        shift_c = off_ref[0, 0, e, 1].astype(F32) + sub_ref[0, 0, e, 1]
        row = lanczos(shift_r - lanes)
        col = lanczos(shift_c + lanes)
        top = halves(skewed(row, half, side, 0))
        bottom = halves(skewed(row, half, side, half - start))
        across = halves(skewed(col, pcols, pcols, 0))
        maps.append((top, bottom, across))

    for e in range(epochs):
        for which in range(3):
            loads[3 * e + which].wait()
        top, bottom, across = maps[e]
        masked = inv_ref[e] * val_ref[e].astype(F32) * cor_ref[0, 0, e].astype(F32)
        stacked = jnp.concatenate([(masked * exp_ref[e]).astype(BF16), masked.astype(BF16)], axis=1)
        upper = dot(top[0], stacked[:side]) + dot(top[1], stacked[:side])
        lower = dot(bottom[0], stacked[start:]) + dot(bottom[1], stacked[start:])
        done = jnp.concatenate([upper.astype(BF16), lower.astype(BF16)], axis=0)
        for plane in range(2):
            part = done[:, plane * pcols : (plane + 1) * pcols]
            warped = dot(part, across[0]) + dot(part, across[1])
            if e == 0:
                tile[plane] = warped
            else:
                tile[plane] += warped

    dec_out[0] = tile[:, 0:BAND, :].astype(BF16)
    dec_out[1] = tile[:, prows - BAND : prows, :].astype(BF16)
    pl.semaphore_wait(barrier, 2 + has_prev.astype(jnp.int32) + has_next.astype(jnp.int32))

    def dec_copy(way):
        return pltpu.make_async_remote_copy(
            src_ref=dec_out.at[way],
            dst_ref=dec_in.at[way],
            send_sem=dec_send.at[way],
            recv_sem=dec_recv.at[way],
            device_id=(me_ra, me_dec + (1 if way else -1)),
            device_id_type=MESH,
        )

    @pl.when(has_prev)
    def _():
        dec_copy(0).start()

    @pl.when(has_next)
    def _():
        dec_copy(1).start()

    side_k = psf_ref.shape[0]
    taps[...] = jnp.zeros_like(taps)
    taps[0:side_k, 0 : psf_ref.shape[1]] = psf_ref[...].astype(F32)
    offset = MARGIN - HALF

    def build(k, carry):
        for s in range(GROUP // 2):
            for parity in range(2):
                row = taps[pl.ds(k * GROUP + 2 * s + parity, 1), :]
                bands[
                    k, parity * LANES : (parity + 1) * LANES, s * 2 * LANES : (s + 1) * 2 * LANES
                ] = skewed(row, LANES, 2 * LANES, offset).astype(BF16)
        return carry

    lax.fori_loop(0, bands.shape[0], build, 0)

    @pl.when(has_next)
    def _():
        dec_copy(0).wait_recv()
        tile[:, prows - 2 * MARGIN : prows - 2 * MARGIN + BAND, :] += dec_in[0].astype(F32)

    @pl.when(has_prev)
    def _():
        dec_copy(1).wait_recv()
        tile[:, 2 * MARGIN - BAND : 2 * MARGIN, :] += dec_in[1].astype(F32)

    low = MARGIN - 32
    high = low + rows + 64
    ra_out[0] = tile[:, low:high, 0:LANES].astype(BF16)
    ra_out[1] = tile[:, low:high, pcols - LANES : pcols].astype(BF16)

    def ra_copy(way):
        return pltpu.make_async_remote_copy(
            src_ref=ra_out.at[way],
            dst_ref=ra_in.at[way],
            send_sem=ra_send.at[way],
            recv_sem=ra_recv.at[way],
            device_id=(next_ra if way else prev_ra, me_dec),
            device_id_type=MESH,
        )

    ra_copy(0).start()
    ra_copy(1).start()
    ra_copy(0).wait_recv()
    tile[:, low:high, pcols - LANES : pcols] += ra_in[0].astype(F32)
    ra_copy(1).wait_recv()
    tile[:, low:high, 0:LANES] += ra_in[1].astype(F32)

    weight_ref[...] = tile[1, MARGIN : MARGIN + rows, MARGIN : MARGIN + cols]
    row_id = lax.broadcasted_iota(jnp.int32, (coadd.shape[0], 1), 0) - MARGIN + me_dec * rows
    inside = (row_id >= 0) & (row_id < n_dec * rows)
    coadd[...] = jnp.where(inside, tile[0] / jnp.maximum(tile[1], 1.0), 0.0)
    deep = shifts.shape[1]
    for s in range(GROUP // 2):
        first = offset + 2 * s
        moved = coadd[first : first + deep, :].astype(BF16)
        for block in range(2):
            shifts[block, :, s * 2 * LANES : (s + 1) * 2 * LANES] = moved[
                :, block * LANES : (block + 2) * LANES
            ]

    tall = rows + GROUP
    total = jnp.zeros((2 * tall, 2 * LANES), F32)
    for k in range(bands.shape[0]):
        pieces = shifts[:, k * GROUP : k * GROUP + tall, :].reshape(2 * tall, shifts.shape[2])
        total = total + dot_t(pieces, bands[k])
    for block in range(2):
        even = total[block * tall : block * tall + rows, :LANES]
        odd = total[block * tall : (block + 1) * tall, LANES:][1 : rows + 1]
        matched_ref[:, block * LANES : (block + 1) * LANES] = even + odd

    @pl.when(has_prev)
    def _():
        dec_copy(0).wait_send()

    @pl.when(has_next)
    def _():
        dec_copy(1).wait_send()

    ra_copy(0).wait_send()
    ra_copy(1).wait_send()


def solution(mesh):
    n_ra, n_dec = mesh.shape["ra"], mesh.shape["dec"]

    def shards(exposures, inv_variance, pixel_valid, correlation, pixel_offset, subpixel, psf_match):
        epochs, prows, pcols = exposures.shape
        rows, cols = prows - 2 * MARGIN, pcols - 2 * MARGIN
        groups = -(-psf_match.shape[0] // GROUP)
        deep = rows + GROUP * groups
        result = jax.ShapeDtypeStruct((rows, cols), F32)
        hbm = pl.BlockSpec(memory_space=pl.ANY)
        smem = pl.BlockSpec(memory_space=pltpu.SMEM)
        vmem = pl.BlockSpec(memory_space=pltpu.VMEM)
        return pl.pallas_call(
            functools.partial(kernel, (epochs, prows, pcols, n_ra, n_dec)),
            out_shape=(result, result),
            in_specs=[hbm, hbm, hbm, smem, smem, smem, vmem],
            out_specs=(vmem, vmem),
            scratch_shapes=[
                pltpu.VMEM((epochs, prows, pcols), F32),
                pltpu.VMEM((epochs, prows, pcols), F32),
                pltpu.VMEM((epochs, prows, pcols), jnp.int32),
                pltpu.VMEM((2, prows, pcols), F32),
                pltpu.VMEM((2, 2, BAND, pcols), BF16),
                pltpu.VMEM((2, 2, BAND, pcols), BF16),
                pltpu.VMEM((2, 2, rows + 64, LANES), BF16),
                pltpu.VMEM((2, 2, rows + 64, LANES), BF16),
                pltpu.VMEM((groups * GROUP, 2 * LANES), F32),
                pltpu.VMEM((groups, 2 * LANES, GROUP * LANES), BF16),
                pltpu.VMEM((prows, pcols), F32),
                pltpu.VMEM((2, deep, GROUP * LANES), BF16),
                pltpu.SemaphoreType.DMA((3 * epochs,)),
                pltpu.SemaphoreType.DMA((2,)),
                pltpu.SemaphoreType.DMA((2,)),
                pltpu.SemaphoreType.DMA((2,)),
                pltpu.SemaphoreType.DMA((2,)),
            ],
            compiler_params=pltpu.CompilerParams(
                collective_id=0, has_side_effects=True, vmem_limit_bytes=48 * 1024 * 1024
            ),
            name="coadd",
        )(exposures, inv_variance, pixel_valid, correlation, pixel_offset, subpixel, psf_match)

    return jax.shard_map(
        shards,
        mesh=mesh,
        in_specs=(
            P(None, "dec", "ra"),
            P(None, "dec", "ra"),
            P(None, "dec", "ra"),
            P("dec", "ra", None),
            P("dec", "ra", None, None),
            P("dec", "ra", None, None),
            P(),
        ),
        out_specs=(P("dec", "ra"), P("dec", "ra")),
        check_vma=False,
    )
```

profile of v0, /device:TPU:1, one launch (start us, length us, event | category | flops | bytes accessed | tf_op | source)
XLA Modules:
  0.0 28.2 jit_solution(2831962475679667162)
XLA Ops:
  0.6 0.0 copy-start
  0.6 1.2 %copy-done = f32[2,320,384]{2,1,0:T(8,128)S(1)} copy-done((f32[2,320,384]{2,1,0:T(8,128)S(1)}, f32[2,320,384]{2,1,0:T(8,128)}, u32[]{:S(2)}) %copy-start) | copy-done | bytes 983064
  1.8 0.0 copy-start.1
  1.8 1.2 %copy-done.1 = f32[2,320,384]{2,1,0:T(8,128)S(1)} copy-done((f32[2,320,384]{2,1,0:T(8,128)S(1)}, f32[2,320,384]{2,1,0:T(8,128)}, u32[]{:S(2)}) %copy-start.1) | copy-done | bytes 983064
  3.0 0.0 copy-start.2
  3.0 1.2 %copy-done.2 = s32[2,320,384]{2,1,0:T(8,128)S(1)} copy-done((s32[2,320,384]{2,1,0:T(8,128)S(1)}, s32[2,320,384]{2,1,0:T(8,128)}, u32[]{:S(2)}) %copy-start.2) | copy-done | bytes 983064
  4.2 0.0 copy-start.3
  4.2 0.7 %copy-done.3 = bf16[63,63]{1,0:T(8,128)(2,1)S(1)} copy-done((bf16[63,63]{1,0:T(8,128)(2,1)S(1)}, bf16[63,63]{1,0:T(8,128)(2,1)}, u32[]{:S(2)}) %copy-start.3) | copy-done | bytes 7962
  5.0 0.0 copy-start.4
  5.0 0.7 %copy-done.4 = s32[1,1,2,2]{3,2,1,0:T(2,128)S(1)} copy-done((s32[1,1,2,2]{3,2,1,0:T(2,128)S(1)}, s32[1,1,2,2]{3,2,1,0:T(2,128)}, u32[]{:S(2)}) %copy-start.4) | copy-done | bytes 40
  5.6 0.0 copy-start.5
  5.6 0.7 %copy-done.5 = f32[1,1,2,2]{3,2,1,0:T(2,128)S(1)} copy-done((f32[1,1,2,2]{3,2,1,0:T(2,128)S(1)}, f32[1,1,2,2]{3,2,1,0:T(2,128)}, u32[]{:S(2)}) %copy-start.5) | copy-done | bytes 40
  6.3 0.0 copy-start.6
  6.3 0.7 %copy-done.6 = s32[1,1,2]{2,1,0:T(1,128)S(1)} copy-done((s32[1,1,2]{2,1,0:T(1,128)S(1)}, s32[1,1,2]{2,1,0:T(1,128)}, u32[]{:S(2)}) %copy-start.6) | copy-done | bytes 32
  7.0 19.9 %coadd.1 = (f32[192,256]{1,0:T(8,128)S(1)}, f32[192,256]{1,0:T(8,128)S(1)}) custom-call(f32[2,320,384]{2,1,0:T(8,128)S(1)} %copy-done, f32[2,320,384]{2,1,0:T(8,128)S(1)} %copy-done.1, s32[2,320,384]{2,1,0:T(8,128)S(1)} %copy-done.2, s32[1,1,2]{2,1,0:T(1,128)S(1)} %copy-done.6, s32[1,1,2,2]{3,2,1,0:T(2,128)S(1)} %copy-done.4, f32[1,1,2,2]{3,2,1,0:T(2,128)S(1)} %copy-done.5, ...), custom_call_target="tpu_custom_call" | custom-call | tf_op jit(solution)/shard_map/coadd/pallas_call | solution.py:258
  26.9 0.7 %copy.11 = f32[192,256]{1,0:T(8,128)} copy(f32[192,256]{1,0:T(8,128)S(1)} %get-tuple-element.4) | data formatting | bytes 393216
  27.5 0.7 %copy.12 = f32[192,256]{1,0:T(8,128)} copy(f32[192,256]{1,0:T(8,128)S(1)} %get-tuple-element.5) | data formatting | bytes 393216
Async XLA Ops:
  0.6 1.2 %copy-start = (f32[2,320,384]{2,1,0:T(8,128)S(1)}, f32[2,320,384]{2,1,0:T(8,128)}, u32[]{:S(2)}) copy-start(f32[2,320,384]{2,1,0:T(8,128)} %exp_hbm.1) | copy-start | bytes 2949124
  1.8 1.2 %copy-start.1 = (f32[2,320,384]{2,1,0:T(8,128)S(1)}, f32[2,320,384]{2,1,0:T(8,128)}, u32[]{:S(2)}) copy-start(f32[2,320,384]{2,1,0:T(8,128)} %inv_hbm.1) | copy-start | bytes 2949124
  3.0 1.2 %copy-start.2 = (s32[2,320,384]{2,1,0:T(8,128)S(1)}, s32[2,320,384]{2,1,0:T(8,128)}, u32[]{:S(2)}) copy-start(s32[2,320,384]{2,1,0:T(8,128)} %val_hbm.1) | copy-start | bytes 2949124
  4.2 0.7 %copy-start.3 = (bf16[63,63]{1,0:T(8,128)(2,1)S(1)}, bf16[63,63]{1,0:T(8,128)(2,1)}, u32[]{:S(2)}) copy-start(bf16[63,63]{1,0:T(8,128)(2,1)} %psf_ref.1) | copy-start | bytes 23818
  5.0 0.7 %copy-start.4 = (s32[1,1,2,2]{3,2,1,0:T(2,128)S(1)}, s32[1,1,2,2]{3,2,1,0:T(2,128)}, u32[]{:S(2)}) copy-start(s32[1,1,2,2]{3,2,1,0:T(2,128)} %off_ref.1) | copy-start | bytes 52
  5.6 0.7 %copy-start.5 = (f32[1,1,2,2]{3,2,1,0:T(2,128)S(1)}, f32[1,1,2,2]{3,2,1,0:T(2,128)}, u32[]{:S(2)}) copy-start(f32[1,1,2,2]{3,2,1,0:T(2,128)} %sub_ref.1) | copy-start | bytes 52
  6.3 0.7 %copy-start.6 = (s32[1,1,2]{2,1,0:T(1,128)S(1)}, s32[1,1,2]{2,1,0:T(1,128)}, u32[]{:S(2)}) copy-start(s32[1,1,2]{2,1,0:T(1,128)} %cor_ref.1) | copy-start | bytes 28
where the time goes:
time: 28.6 us; the launch traced here: 28.2 us
  Pallas kernels  19.9 us (70%)
  local copies, waits for them, and re-layouts  7.68 us (27%)
  between operations  0.66 us (2%)
    pallas_call x1, Pallas kernels, shards(): pl.pallas_call(functools.partial(kernel, (epochs, prows, pcols, n_ra, n_d...  19.9 us
    unnamed x16, local copies, waits for them, and re-layouts  7.68 us

commit v1 on v0

--- a/solution.py
+++ b/solution.py
@@ -55,29 +55,38 @@
     exp_hbm,
     inv_hbm,
     val_hbm,
-    cor_ref,
-    off_ref,
-    sub_ref,
-    psf_ref,
+    cor_hbm,
+    off_hbm,
+    sub_hbm,
+    psf_hbm,
     matched_ref,
     weight_ref,
     exp_ref,
     inv_ref,
     val_ref,
+    cor_ref,
+    off_ref,
+    sub_ref,
+    psf_ref,
     tile,
     dec_out,
     dec_in,
-    ra_out,
-    ra_in,
+    mid_out,
+    mid_in,
+    edge_out,
+    edge_in,
     taps,
     bands,
     coadd,
     shifts,
+    small_sem,
     load_sem,
     dec_send,
     dec_recv,
-    ra_send,
-    ra_recv,
+    mid_send,
+    mid_recv,
+    edge_send,
+    edge_recv,
 ):
     epochs, prows, pcols, n_ra, n_dec = dims
     rows, cols = prows - 2 * MARGIN, pcols - 2 * MARGIN
@@ -85,13 +94,19 @@
     prev_ra, next_ra = lax.rem(me_ra + n_ra - 1, n_ra), lax.rem(me_ra + 1, n_ra)
     has_prev, has_next = me_dec > 0, me_dec < n_dec - 1
 
+    small = [
+        pltpu.make_async_copy(src, dst, small_sem.at[i])
+        for i, (src, dst) in enumerate(
+            ((off_hbm, off_ref), (sub_hbm, sub_ref), (cor_hbm, cor_ref), (psf_hbm, psf_ref))
+        )
+    ]
     loads = []
     for e in range(epochs):
         for which, (src, dst) in enumerate(
-            ((exp_hbm, exp_ref), (inv_hbm, inv_ref), (val_hbm, val_ref))
+            ((inv_hbm, inv_ref), (val_hbm, val_ref), (exp_hbm, exp_ref))
         ):
             loads.append(pltpu.make_async_copy(src.at[e], dst.at[e], load_sem.at[3 * e + which]))
-    for copy in loads:
+    for copy in small + loads:
         copy.start()
 
     barrier = pltpu.get_barrier_semaphore()
@@ -106,40 +121,66 @@
     def _():
         pl.semaphore_signal(barrier, inc=1, device_id=(me_ra, me_dec + 1), device_id_type=MESH)
 
-    half = prows // 2
-    side = 256
-    start = prows - side
-    maps = []
+    for copy in small[:3]:
+        copy.wait()
+    inner = prows - 2 * BAND
+    side = 2 * LANES
+    start = (prows - side) // 2
+    row_maps, col_maps = [], []
     for e in range(epochs):
         lanes = signed_lanes(512)
         shift_r = off_ref[0, 0, e, 0].astype(F32) + sub_ref[0, 0, e, 0]
         shift_c = off_ref[0, 0, e, 1].astype(F32) + sub_ref[0, 0, e, 1]
         row = lanczos(shift_r - lanes)
         col = lanczos(shift_c + lanes)
-        top = halves(skewed(row, half, side, 0))
-        bottom = halves(skewed(row, half, side, half - start))
+        top = jnp.concatenate(halves(skewed(row, BAND, LANES, 0)), axis=1)
+        bottom = jnp.concatenate(halves(skewed(row, BAND, LANES, LANES - BAND)), axis=1)
+        middle = jnp.concatenate(halves(skewed(row, inner, side, BAND - start)), axis=0)
+        row_maps.append((top, bottom, middle))
         across = halves(skewed(col, pcols, pcols, 0))
-        maps.append((top, bottom, across))
-
+        col_maps.append(across)
+    spans = ((0, 2 * LANES), (0, pcols), (pcols - 2 * LANES, pcols))
+    col_blocks = []
+    for block, (first, last) in enumerate(spans):
+        picked = slice(block * LANES, (block + 1) * LANES)
+        col_blocks.append(
+            jnp.concatenate(
+                [
+                    jnp.concatenate([part[first:last, picked] for part in across], axis=1)
+                    for across in col_maps
+                ],
+                axis=0,
+            )
+        )
+
+    def column_pass(pieces):
+        stacked = [jnp.concatenate([p[:, :pcols], p[:, pcols:]], axis=0) for p in pieces]
+        out = []
+        for block, (first, last) in enumerate(spans):
+            both = dot(jnp.concatenate([p[:, first:last] for p in stacked], axis=1), col_blocks[block])
+            out.append(both[:, :LANES] + both[:, LANES:])
+        return out
+
+    rim_rows, inner_rows = [], []
     for e in range(epochs):
         for which in range(3):
             loads[3 * e + which].wait()
-        top, bottom, across = maps[e]
+        top, bottom, middle = row_maps[e]
         masked = inv_ref[e] * val_ref[e].astype(F32) * cor_ref[0, 0, e].astype(F32)
-        stacked = jnp.concatenate([(masked * exp_ref[e]).astype(BF16), masked.astype(BF16)], axis=1)
-        upper = dot(top[0], stacked[:side]) + dot(top[1], stacked[:side])
-        lower = dot(bottom[0], stacked[start:]) + dot(bottom[1], stacked[start:])
-        done = jnp.concatenate([upper.astype(BF16), lower.astype(BF16)], axis=0)
+        pixels = jnp.concatenate([(masked * exp_ref[e]).astype(BF16), masked.astype(BF16)], axis=1)
+        upper = dot(top, jnp.concatenate([pixels[:LANES]] * 2, axis=0))
+        lower = dot(bottom, jnp.concatenate([pixels[prows - LANES :]] * 2, axis=0))
+        rim_rows.append(jnp.concatenate([upper.astype(BF16), lower.astype(BF16)], axis=0))
+        both = dot(middle, pixels[start : start + side])
+        inner_rows.append((both[:inner] + both[inner:]).astype(BF16))
+
+    for block, value in enumerate(column_pass(rim_rows)):
+        where = slice(block * LANES, (block + 1) * LANES)
         for plane in range(2):
-            part = done[:, plane * pcols : (plane + 1) * pcols]
-            warped = dot(part, across[0]) + dot(part, across[1])
-            if e == 0:
-                tile[plane] = warped
-            else:
-                tile[plane] += warped
-
-    dec_out[0] = tile[:, 0:BAND, :].astype(BF16)
-    dec_out[1] = tile[:, prows - BAND : prows, :].astype(BF16)
+            for way in range(2):
+                part = value[(2 * plane + way) * BAND : (2 * plane + way + 1) * BAND]
+                tile[plane, way * (prows - BAND) : way * (prows - BAND) + BAND, where] = part
+                dec_out[way, plane, :, where] = part.astype(BF16)
     pl.semaphore_wait(barrier, 2 + has_prev.astype(jnp.int32) + has_next.astype(jnp.int32))
 
     def dec_copy(way):
@@ -152,6 +193,26 @@
             device_id_type=MESH,
         )
 
+    def mid_copy(way):
+        return pltpu.make_async_remote_copy(
+            src_ref=mid_out.at[way],
+            dst_ref=mid_in.at[way],
+            send_sem=mid_send.at[way],
+            recv_sem=mid_recv.at[way],
+            device_id=(next_ra if way else prev_ra, me_dec),
+            device_id_type=MESH,
+        )
+
+    def edge_copy(way, part):
+        return pltpu.make_async_remote_copy(
+            src_ref=edge_out.at[way, part],
+            dst_ref=edge_in.at[way, part],
+            send_sem=edge_send.at[way, part],
+            recv_sem=edge_recv.at[way, part],
+            device_id=(next_ra if way else prev_ra, me_dec),
+            device_id_type=MESH,
+        )
+
     @pl.when(has_prev)
     def _():
         dec_copy(0).start()
@@ -160,6 +221,19 @@
     def _():
         dec_copy(1).start()
 
+    for block, value in enumerate(column_pass(inner_rows)):
+        where = slice(block * LANES, (block + 1) * LANES)
+        for plane in range(2):
+            tile[plane, BAND : BAND + inner, where] = value[plane * inner : (plane + 1) * inner]
+
+    ends = (slice(0, LANES), slice(pcols - LANES, pcols))
+    core = slice(2 * MARGIN, prows - 2 * MARGIN)
+    for way in range(2):
+        mid_out[way] = tile[:, core, ends[way]].astype(BF16)
+    for way in range(2):
+        mid_copy(way).start()
+
+    small[3].wait()
     side_k = psf_ref.shape[0]
     taps[...] = jnp.zeros_like(taps)
     taps[0:side_k, 0 : psf_ref.shape[1]] = psf_ref[...].astype(F32)
@@ -176,37 +250,29 @@
 
     lax.fori_loop(0, bands.shape[0], build, 0)
 
-    @pl.when(has_next)
-    def _():
-        dec_copy(0).wait_recv()
-        tile[:, prows - 2 * MARGIN : prows - 2 * MARGIN + BAND, :] += dec_in[0].astype(F32)
-
-    @pl.when(has_prev)
-    def _():
-        dec_copy(1).wait_recv()
-        tile[:, 2 * MARGIN - BAND : 2 * MARGIN, :] += dec_in[1].astype(F32)
-
-    low = MARGIN - 32
-    high = low + rows + 64
-    ra_out[0] = tile[:, low:high, 0:LANES].astype(BF16)
-    ra_out[1] = tile[:, low:high, pcols - LANES : pcols].astype(BF16)
-
-    def ra_copy(way):
-        return pltpu.make_async_remote_copy(
-            src_ref=ra_out.at[way],
-            dst_ref=ra_in.at[way],
-            send_sem=ra_send.at[way],
-            recv_sem=ra_recv.at[way],
-            device_id=(next_ra if way else prev_ra, me_dec),
-            device_id_type=MESH,
-        )
-
-    ra_copy(0).start()
-    ra_copy(1).start()
-    ra_copy(0).wait_recv()
-    tile[:, low:high, pcols - LANES : pcols] += ra_in[0].astype(F32)
-    ra_copy(1).wait_recv()
-    tile[:, low:high, 0:LANES] += ra_in[1].astype(F32)
+    edges = (
+        slice(2 * MARGIN - BAND, 2 * MARGIN),
+        slice(prows - 2 * MARGIN, prows - 2 * MARGIN + BAND),
+    )
+    for part, present in ((0, has_prev), (1, has_next)):
+
+        @pl.when(present)
+        def _():
+            dec_copy(1 - part).wait_recv()
+            tile[:, edges[part], :] += dec_in[1 - part].astype(F32)
+
+        for way in range(2):
+            edge_out[way, part] = tile[:, edges[part], ends[way]].astype(BF16)
+        for way in range(2):
+            edge_copy(way, part).start()
+
+    for way in range(2):
+        mid_copy(way).wait_recv()
+        tile[:, core, ends[1 - way]] += mid_in[way].astype(F32)
+    for part in range(2):
+        for way in range(2):
+            edge_copy(way, part).wait_recv()
+            tile[:, edges[part], ends[1 - way]] += edge_in[way, part].astype(F32)
 
     weight_ref[...] = tile[1, MARGIN : MARGIN + rows, MARGIN : MARGIN + cols]
     row_id = lax.broadcasted_iota(jnp.int32, (coadd.shape[0], 1), 0) - MARGIN + me_dec * rows
@@ -239,8 +305,10 @@
     def _():
         dec_copy(1).wait_send()
 
-    ra_copy(0).wait_send()
-    ra_copy(1).wait_send()
+    for way in range(2):
+        mid_copy(way).wait_send()
+        for part in range(2):
+            edge_copy(way, part).wait_send()
 
 
 def solution(mesh):
@@ -252,38 +320,46 @@
         groups = -(-psf_match.shape[0] // GROUP)
         deep = rows + GROUP * groups
         result = jax.ShapeDtypeStruct((rows, cols), F32)
-        hbm = pl.BlockSpec(memory_space=pl.ANY)
-        smem = pl.BlockSpec(memory_space=pltpu.SMEM)
+        hbm = pl.BlockSpec(memory_space=pltpu.HBM)
         vmem = pl.BlockSpec(memory_space=pltpu.VMEM)
         return pl.pallas_call(
             functools.partial(kernel, (epochs, prows, pcols, n_ra, n_dec)),
             out_shape=(result, result),
-            in_specs=[hbm, hbm, hbm, smem, smem, smem, vmem],
+            in_specs=[hbm] * 7,
             out_specs=(vmem, vmem),
             scratch_shapes=[
                 pltpu.VMEM((epochs, prows, pcols), F32),
                 pltpu.VMEM((epochs, prows, pcols), F32),
                 pltpu.VMEM((epochs, prows, pcols), jnp.int32),
+                pltpu.SMEM(correlation.shape, jnp.int32),
+                pltpu.SMEM(pixel_offset.shape, jnp.int32),
+                pltpu.SMEM(subpixel.shape, F32),
+                pltpu.VMEM(psf_match.shape, BF16),
                 pltpu.VMEM((2, prows, pcols), F32),
                 pltpu.VMEM((2, 2, BAND, pcols), BF16),
                 pltpu.VMEM((2, 2, BAND, pcols), BF16),
-                pltpu.VMEM((2, 2, rows + 64, LANES), BF16),
-                pltpu.VMEM((2, 2, rows + 64, LANES), BF16),
+                pltpu.VMEM((2, 2, prows - 4 * MARGIN, LANES), BF16),
+                pltpu.VMEM((2, 2, prows - 4 * MARGIN, LANES), BF16),
+                pltpu.VMEM((2, 2, 2, BAND, LANES), BF16),
+                pltpu.VMEM((2, 2, 2, BAND, LANES), BF16),
                 pltpu.VMEM((groups * GROUP, 2 * LANES), F32),
                 pltpu.VMEM((groups, 2 * LANES, GROUP * LANES), BF16),
                 pltpu.VMEM((prows, pcols), F32),
                 pltpu.VMEM((2, deep, GROUP * LANES), BF16),
+                pltpu.SemaphoreType.DMA((4,)),
                 pltpu.SemaphoreType.DMA((3 * epochs,)),
                 pltpu.SemaphoreType.DMA((2,)),
                 pltpu.SemaphoreType.DMA((2,)),
                 pltpu.SemaphoreType.DMA((2,)),
                 pltpu.SemaphoreType.DMA((2,)),
+                pltpu.SemaphoreType.DMA((2, 2)),
+                pltpu.SemaphoreType.DMA((2, 2)),
             ],
             compiler_params=pltpu.CompilerParams(
                 collective_id=0, has_side_effects=True, vmem_limit_bytes=48 * 1024 * 1024
             ),
             name="coadd",
-        )(exposures, inv_variance, pixel_valid, correlation, pixel_offset, subpixel, psf_match)
+        )(*[pltpu.with_memory_space_constraint(x, pltpu.HBM) for x in (exposures, inv_variance, pixel_valid, correlation, pixel_offset, subpixel, psf_match)])
 
     return jax.shard_map(
         shards,

time: 28.6 us -> 18.8 us (0.66)
  local copies, waits for them, and re-layouts: 7.68 us -> 1.36 us
  Pallas kernels: 19.9 us -> 16.7 us
    unnamed x16 -> x2, local copies, waits for them, and re-layouts: 7.68 us -> 1.36 us
    pallas_call x1, Pallas kernels: 19.9 us -> 16.7 us  [shards(): pl.pallas_call(functools.partial(kernel, (epochs, prows, pcols, n_ra, n_d...]
where the time goes in v1:
time: 18.8 us; the launch traced here: 18.7 us
  Pallas kernels  16.7 us (89%)
  local copies, waits for them, and re-layouts  1.36 us (7%)
  between operations  0.64 us (3%)
    pallas_call x1, Pallas kernels, shards(): pl.pallas_call(functools.partial(kernel, (epochs, prows, pcols, n_ra, n_d...  16.7 us
    unnamed x2, local copies, waits for them, and re-layouts  1.36 us

profile of v1, /device:TPU:1, one launch (start us, length us, event | category | flops | bytes accessed | tf_op | source)
XLA Modules:
  0.0 18.7 jit_solution(9781395752181797973)
XLA Ops:
  0.6 16.7 %coadd.1 = (f32[192,256]{1,0:T(8,128)S(1)}, f32[192,256]{1,0:T(8,128)S(1)}) custom-call(f32[2,320,384]{2,1,0:T(8,128)} %exp_hbm.1, f32[2,320,384]{2,1,0:T(8,128)} %inv_hbm.1, s32[2,320,384]{2,1,0:T(8,128)} %val_hbm.1, s32[1,1,2]{2,1,0:T(1,128)} %cor_hbm.1, s32[1,1,2,2]{3,2,1,0:T(2,128)} %off_hbm.1, f32[1,1,2,2]{3,2,1,0:T(2,128)} %sub_hbm.1, ...), custom_call_target="tpu_custom_call" | custom-call | tf_op jit(solution)/shard_map/coadd/pallas_call | solution.py:325
  17.3 0.7 %copy.11 = f32[192,256]{1,0:T(8,128)} copy(f32[192,256]{1,0:T(8,128)S(1)} %get-tuple-element.4) | data formatting | bytes 393216
  18.0 0.7 %copy.12 = f32[192,256]{1,0:T(8,128)} copy(f32[192,256]{1,0:T(8,128)S(1)} %get-tuple-element.5) | data formatting | bytes 393216

commit v2 on v1

--- a/solution.py
+++ b/solution.py
@@ -69,8 +69,11 @@
     sub_ref,
     psf_ref,
     tile,
+    slab,
     dec_out,
     dec_in,
+    dec_core_out,
+    dec_core_in,
     mid_out,
     mid_in,
     edge_out,
@@ -79,10 +82,13 @@
     bands,
     coadd,
     shifts,
+    inner_sum,
     small_sem,
     load_sem,
     dec_send,
     dec_recv,
+    dec_core_send,
+    dec_core_recv,
     mid_send,
     mid_recv,
     edge_send,
@@ -171,8 +177,7 @@
         upper = dot(top, jnp.concatenate([pixels[:LANES]] * 2, axis=0))
         lower = dot(bottom, jnp.concatenate([pixels[prows - LANES :]] * 2, axis=0))
         rim_rows.append(jnp.concatenate([upper.astype(BF16), lower.astype(BF16)], axis=0))
-        both = dot(middle, pixels[start : start + side])
-        inner_rows.append((both[:inner] + both[inner:]).astype(BF16))
+        slab[e] = pixels[start : start + side]
 
     for block, value in enumerate(column_pass(rim_rows)):
         where = slice(block * LANES, (block + 1) * LANES)
@@ -180,7 +185,12 @@
             for way in range(2):
                 part = value[(2 * plane + way) * BAND : (2 * plane + way + 1) * BAND]
                 tile[plane, way * (prows - BAND) : way * (prows - BAND) + BAND, where] = part
-                dec_out[way, plane, :, where] = part.astype(BF16)
+                if block == 1:
+                    dec_core_out[way, plane] = part.astype(BF16)
+                else:
+                    dec_out[way, plane, :, block // 2 * LANES : (block // 2 + 1) * LANES] = (
+                        part.astype(BF16)
+                    )
     pl.semaphore_wait(barrier, 2 + has_prev.astype(jnp.int32) + has_next.astype(jnp.int32))
 
     def dec_copy(way):
@@ -193,6 +203,16 @@
             device_id_type=MESH,
         )
 
+    def dec_core_copy(way):
+        return pltpu.make_async_remote_copy(
+            src_ref=dec_core_out.at[way],
+            dst_ref=dec_core_in.at[way],
+            send_sem=dec_core_send.at[way],
+            recv_sem=dec_core_recv.at[way],
+            device_id=(me_ra, me_dec + (1 if way else -1)),
+            device_id_type=MESH,
+        )
+
     def mid_copy(way):
         return pltpu.make_async_remote_copy(
             src_ref=mid_out.at[way],
@@ -216,11 +236,16 @@
     @pl.when(has_prev)
     def _():
         dec_copy(0).start()
+        dec_core_copy(0).start()
 
     @pl.when(has_next)
     def _():
         dec_copy(1).start()
-
+        dec_core_copy(1).start()
+
+    for e in range(epochs):
+        both = dot(row_maps[e][2], slab[e])
+        inner_rows.append((both[:inner] + both[inner:]).astype(BF16))
     for block, value in enumerate(column_pass(inner_rows)):
         where = slice(block * LANES, (block + 1) * LANES)
         for plane in range(2):
@@ -243,9 +268,12 @@
         for s in range(GROUP // 2):
             for parity in range(2):
                 row = taps[pl.ds(k * GROUP + 2 * s + parity, 1), :]
-                bands[
-                    k, parity * LANES : (parity + 1) * LANES, s * 2 * LANES : (s + 1) * 2 * LANES
-                ] = skewed(row, LANES, 2 * LANES, offset).astype(BF16)
+                matrix = skewed(row, LANES, 2 * LANES, offset).astype(BF16)
+                for end in range(2):
+                    first = (2 * end + parity) * LANES
+                    bands[k, first : first + LANES, s * LANES : (s + 1) * LANES] = matrix[
+                        :, (1 - end) * LANES : (2 - end) * LANES
+                    ]
         return carry
 
     lax.fori_loop(0, bands.shape[0], build, 0)
@@ -259,56 +287,83 @@
         @pl.when(present)
         def _():
             dec_copy(1 - part).wait_recv()
-            tile[:, edges[part], :] += dec_in[1 - part].astype(F32)
+            for end in range(2):
+                tile[:, edges[part], ends[end]] += dec_in[
+                    1 - part, :, :, end * LANES : (end + 1) * LANES
+                ].astype(F32)
 
         for way in range(2):
             edge_out[way, part] = tile[:, edges[part], ends[way]].astype(BF16)
         for way in range(2):
             edge_copy(way, part).start()
 
+    row_id = lax.broadcasted_iota(jnp.int32, (prows, 1), 0) - MARGIN + me_dec * rows
+    inside = (row_id >= 0) & (row_id < n_dec * rows)
+    deep, tall = shifts.shape[1], rows + GROUP
+
+    def match(slot, where, chosen):
+        coadd[:, where] = jnp.where(
+            inside, tile[0, :, where] / jnp.maximum(tile[1, :, where], 1.0), 0.0
+        )
+        for s in range(GROUP // 2):
+            first = offset + 2 * s
+            shifts[slot, :, s * LANES : (s + 1) * LANES] = coadd[
+                first : first + deep, where
+            ].astype(BF16)
+        total = None
+        for k in range(bands.shape[0]):
+            part = dot_t(shifts[slot, k * GROUP : k * GROUP + tall, :], bands[k, chosen, :])
+            total = part if total is None else total + part
+        return total
+
+    for part, present in ((0, has_prev), (1, has_next)):
+
+        @pl.when(present)
+        def _():
+            dec_core_copy(1 - part).wait_recv()
+            tile[:, edges[part], LANES : 2 * LANES] += dec_core_in[1 - part].astype(F32)
+
+    inner_sum[...] = match(2, slice(LANES, 2 * LANES), slice(0, 4 * LANES))
+
     for way in range(2):
         mid_copy(way).wait_recv()
         tile[:, core, ends[1 - way]] += mid_in[way].astype(F32)
-    for part in range(2):
-        for way in range(2):
-            edge_copy(way, part).wait_recv()
-            tile[:, edges[part], ends[1 - way]] += edge_in[way, part].astype(F32)
-
+    for end in range(2):
+        for part in range(2):
+            edge_copy(1 - end, part).wait_recv()
+            tile[:, edges[part], ends[end]] += edge_in[1 - end, part].astype(F32)
+        total = match(end, ends[end], slice((1 - end) * 2 * LANES, (2 - end) * 2 * LANES))
+        total = total + inner_sum[:, end * 2 * LANES : (end + 1) * 2 * LANES]
+        matched_ref[:, end * LANES : (end + 1) * LANES] = (
+            total[:rows, :LANES] + total[1 : rows + 1, LANES:]
+        )
     weight_ref[...] = tile[1, MARGIN : MARGIN + rows, MARGIN : MARGIN + cols]
-    row_id = lax.broadcasted_iota(jnp.int32, (coadd.shape[0], 1), 0) - MARGIN + me_dec * rows
-    inside = (row_id >= 0) & (row_id < n_dec * rows)
-    coadd[...] = jnp.where(inside, tile[0] / jnp.maximum(tile[1], 1.0), 0.0)
-    deep = shifts.shape[1]
-    for s in range(GROUP // 2):
-        first = offset + 2 * s
-        moved = coadd[first : first + deep, :].astype(BF16)
-        for block in range(2):
-            shifts[block, :, s * 2 * LANES : (s + 1) * 2 * LANES] = moved[
-                :, block * LANES : (block + 2) * LANES
-            ]
-
-    tall = rows + GROUP
-    total = jnp.zeros((2 * tall, 2 * LANES), F32)
-    for k in range(bands.shape[0]):
-        pieces = shifts[:, k * GROUP : k * GROUP + tall, :].reshape(2 * tall, shifts.shape[2])
-        total = total + dot_t(pieces, bands[k])
-    for block in range(2):
-        even = total[block * tall : block * tall + rows, :LANES]
-        odd = total[block * tall : (block + 1) * tall, LANES:][1 : rows + 1]
-        matched_ref[:, block * LANES : (block + 1) * LANES] = even + odd
 
     @pl.when(has_prev)
     def _():
         dec_copy(0).wait_send()
+        dec_core_copy(0).wait_send()
 
     @pl.when(has_next)
     def _():
         dec_copy(1).wait_send()
+        dec_core_copy(1).wait_send()
 
     for way in range(2):
         mid_copy(way).wait_send()
         for part in range(2):
             edge_copy(way, part).wait_send()
+
+
+def finish(matched_in, weight_in, matched_out, weight_out, sems):
+    copies = [
+        pltpu.make_async_copy(matched_in, matched_out, sems.at[0]),
+        pltpu.make_async_copy(weight_in, weight_out, sems.at[1]),
+    ]
+    for copy in copies:
+        copy.start()
+    for copy in copies:
+        copy.wait()
 
 
 def solution(mesh):
@@ -322,7 +377,7 @@
         result = jax.ShapeDtypeStruct((rows, cols), F32)
         hbm = pl.BlockSpec(memory_space=pltpu.HBM)
         vmem = pl.BlockSpec(memory_space=pltpu.VMEM)
-        return pl.pallas_call(
+        sums = pl.pallas_call(
             functools.partial(kernel, (epochs, prows, pcols, n_ra, n_dec)),
             out_shape=(result, result),
             in_specs=[hbm] * 7,
@@ -336,18 +391,24 @@
                 pltpu.SMEM(subpixel.shape, F32),
                 pltpu.VMEM(psf_match.shape, BF16),
                 pltpu.VMEM((2, prows, pcols), F32),
-                pltpu.VMEM((2, 2, BAND, pcols), BF16),
-                pltpu.VMEM((2, 2, BAND, pcols), BF16),
+                pltpu.VMEM((epochs, 2 * LANES, 2 * pcols), BF16),
+                pltpu.VMEM((2, 2, BAND, 2 * LANES), BF16),
+                pltpu.VMEM((2, 2, BAND, 2 * LANES), BF16),
+                pltpu.VMEM((2, 2, BAND, LANES), BF16),
+                pltpu.VMEM((2, 2, BAND, LANES), BF16),
                 pltpu.VMEM((2, 2, prows - 4 * MARGIN, LANES), BF16),
                 pltpu.VMEM((2, 2, prows - 4 * MARGIN, LANES), BF16),
                 pltpu.VMEM((2, 2, 2, BAND, LANES), BF16),
                 pltpu.VMEM((2, 2, 2, BAND, LANES), BF16),
                 pltpu.VMEM((groups * GROUP, 2 * LANES), F32),
-                pltpu.VMEM((groups, 2 * LANES, GROUP * LANES), BF16),
+                pltpu.VMEM((groups, 4 * LANES, GROUP // 2 * LANES), BF16),
                 pltpu.VMEM((prows, pcols), F32),
-                pltpu.VMEM((2, deep, GROUP * LANES), BF16),
+                pltpu.VMEM((3, deep, GROUP // 2 * LANES), BF16),
+                pltpu.VMEM((rows + GROUP, 4 * LANES), F32),
                 pltpu.SemaphoreType.DMA((4,)),
                 pltpu.SemaphoreType.DMA((3 * epochs,)),
+                pltpu.SemaphoreType.DMA((2,)),
+                pltpu.SemaphoreType.DMA((2,)),
                 pltpu.SemaphoreType.DMA((2,)),
                 pltpu.SemaphoreType.DMA((2,)),
                 pltpu.SemaphoreType.DMA((2,)),
@@ -360,6 +421,15 @@
             ),
             name="coadd",
         )(*[pltpu.with_memory_space_constraint(x, pltpu.HBM) for x in (exposures, inv_variance, pixel_valid, correlation, pixel_offset, subpixel, psf_match)])
+        return pl.pallas_call(
+            finish,
+            out_shape=(result, result),
+            in_specs=[vmem, vmem],
+            out_specs=(hbm, hbm),
+            scratch_shapes=[pltpu.SemaphoreType.DMA((2,))],
+            compiler_params=pltpu.CompilerParams(vmem_limit_bytes=1024 * 1024),
+            name="finish",
+        )(*sums)
 
     return jax.shard_map(
         shards,

time: 18.8 us -> 17.9 us (0.952)
  local copies, waits for them, and re-layouts: 1.36 us -> 0 us
  Pallas kernels: 16.7 us -> 17.1 us
    unnamed x2 -> x0, local copies, waits for them, and re-layouts: 1.36 us -> none
    pallas_call x0 -> x1, Pallas kernels: none -> 0.76 us  [shards(): pl.pallas_call(finish, out_shape=(result, result), in_specs=[vmem, vmem],...]
    pallas_call x1, Pallas kernels: 16.7 us -> 16.4 us  [shards(): pl.pallas_call(functools.partial(kernel, (epochs, prows, pcols, n_ra, n_d...]
where the time goes in v2:
time: 17.9 us; the launch traced here: 17.8 us
  Pallas kernels  17.1 us (96%)
  between operations  0.64 us (4%)
    pallas_call x1, Pallas kernels, shards(): pl.pallas_call(functools.partial(kernel, (epochs, prows, pcols, n_ra, n_d...  16.4 us
    pallas_call x1, Pallas kernels, shards(): pl.pallas_call(finish, out_shape=(result, result), in_specs=[vmem, vmem],...  0.76 us

profile of v2, /device:TPU:1, one launch (start us, length us, event | category | flops | bytes accessed | tf_op | source)
XLA Modules:
  0.0 17.8 jit_solution(9214538455445300336)
XLA Ops:
  0.6 16.4 %coadd.1 = (f32[192,256]{1,0:T(8,128)S(1)}, f32[192,256]{1,0:T(8,128)S(1)}) custom-call(f32[2,320,384]{2,1,0:T(8,128)} %exp_hbm.1, f32[2,320,384]{2,1,0:T(8,128)} %inv_hbm.1, s32[2,320,384]{2,1,0:T(8,128)} %val_hbm.1, s32[1,1,2]{2,1,0:T(1,128)} %cor_hbm.1, s32[1,1,2,2]{3,2,1,0:T(2,128)} %off_hbm.1, f32[1,1,2,2]{3,2,1,0:T(2,128)} %sub_hbm.1, ...), custom_call_target="tpu_custom_call" | custom-call | tf_op jit(solution)/shard_map/coadd/pallas_call | solution.py:380
  17.0 0.8 %finish.1 = (f32[192,256]{1,0:T(8,128)}, f32[192,256]{1,0:T(8,128)}) custom-call(f32[192,256]{1,0:T(8,128)S(1)} %get-tuple-element.4.matched_in, f32[192,256]{1,0:T(8,128)S(1)} %get-tuple-element.5.weight_in), custom_call_target="tpu_custom_call" | custom-call | tf_op jit(solution)/shard_map/finish/pallas_call | solution.py:424

commit v3 on v2

--- a/solution.py
+++ b/solution.py
@@ -43,6 +43,35 @@
 def halves(value):
     high = value.astype(BF16)
     return high, (value - high.astype(F32)).astype(BF16)
+
+
+def lane_ids(value):
+    return lax.broadcasted_iota(jnp.int32, value.shape, 1)
+
+
+def packed(planes, way):
+    first, second = planes[0], planes[1]
+    if way:
+        first, second = pltpu.roll(first, BAND, 1), pltpu.roll(second, BAND, 1)
+    half = first.shape[0] // 2
+    upper = jnp.where(lane_ids(first) < BAND, first, pltpu.roll(second, LANES - BAND, 1))
+    low, high = second[:half], second[half:]
+    lower = jnp.where(lane_ids(low) < LANES // 2, low, pltpu.roll(high, LANES // 2, 1))
+    return jnp.concatenate([upper, lower], axis=0).astype(BF16)
+
+
+def unpacked(value, way):
+    value = value.astype(F32)
+    half = value.shape[0] // 3
+    upper, lower = value[: 2 * half], value[2 * half :]
+    lanes = lane_ids(upper)
+    first = jnp.where(lanes < BAND, upper, 0.0)
+    low = jnp.concatenate([lower, pltpu.roll(lower, LANES // 2, 1)], axis=0)
+    high = jnp.where(lanes < BAND, pltpu.roll(upper, BAND, 1), 0.0)
+    second = jnp.where(lanes < LANES // 2, low, high)
+    if way:
+        first, second = pltpu.roll(first, LANES - BAND, 1), pltpu.roll(second, LANES - BAND, 1)
+    return first, second
 
 
 def signed_lanes(width):
@@ -106,12 +135,21 @@
             ((off_hbm, off_ref), (sub_hbm, sub_ref), (cor_hbm, cor_ref), (psf_hbm, psf_ref))
         )
     ]
-    loads = []
-    for e in range(epochs):
-        for which, (src, dst) in enumerate(
-            ((inv_hbm, inv_ref), (val_hbm, val_ref), (exp_hbm, exp_ref))
-        ):
-            loads.append(pltpu.make_async_copy(src.at[e], dst.at[e], load_sem.at[3 * e + which]))
+    segments = (
+        slice(0, LANES),
+        slice(prows - LANES, prows),
+        slice(LANES, prows - LANES),
+    )
+
+    def load(e, segment, which):
+        src, dst = ((inv_hbm, inv_ref), (val_hbm, val_ref), (exp_hbm, exp_ref))[which]
+        return pltpu.make_async_copy(
+            src.at[e, segments[segment]], dst.at[e, segments[segment]], load_sem.at[e, segment, which]
+        )
+
+    order = [(e, segment) for e in range(epochs) for segment in range(2)]
+    order += [(e, 2) for e in range(epochs)]
+    loads = [load(e, segment, which) for e, segment in order for which in range(3)]
     for copy in small + loads:
         copy.start()
 
@@ -168,16 +206,26 @@
         return out
 
     rim_rows, inner_rows = [], []
+    def pixels(e, segment):
+        for which in range(3):
+            load(e, segment, which).wait()
+        at = segments[segment]
+        masked = inv_ref[e, at] * val_ref[e, at].astype(F32) * cor_ref[0, 0, e].astype(F32)
+        return jnp.concatenate([(masked * exp_ref[e, at]).astype(BF16), masked.astype(BF16)], axis=1)
+
+    reach = LANES - start
     for e in range(epochs):
-        for which in range(3):
-            loads[3 * e + which].wait()
-        top, bottom, middle = row_maps[e]
-        masked = inv_ref[e] * val_ref[e].astype(F32) * cor_ref[0, 0, e].astype(F32)
-        pixels = jnp.concatenate([(masked * exp_ref[e]).astype(BF16), masked.astype(BF16)], axis=1)
-        upper = dot(top, jnp.concatenate([pixels[:LANES]] * 2, axis=0))
-        lower = dot(bottom, jnp.concatenate([pixels[prows - LANES :]] * 2, axis=0))
-        rim_rows.append(jnp.concatenate([upper.astype(BF16), lower.astype(BF16)], axis=0))
-        slab[e] = pixels[start : start + side]
+        rims = []
+        for segment in range(2):
+            part = pixels(e, segment)
+            rims.append(
+                dot(row_maps[e][segment], jnp.concatenate([part, part], axis=0)).astype(BF16)
+            )
+            if segment:
+                slab[e, side - reach : side] = part[:reach]
+            else:
+                slab[e, 0:reach] = part[start:]
+        rim_rows.append(jnp.concatenate(rims, axis=0))
 
     for block, value in enumerate(column_pass(rim_rows)):
         where = slice(block * LANES, (block + 1) * LANES)
@@ -244,6 +292,7 @@
         dec_core_copy(1).start()
 
     for e in range(epochs):
+        slab[e, reach : side - reach] = pixels(e, 2)
         both = dot(row_maps[e][2], slab[e])
         inner_rows.append((both[:inner] + both[inner:]).astype(BF16))
     for block, value in enumerate(column_pass(inner_rows)):
@@ -254,7 +303,7 @@
     ends = (slice(0, LANES), slice(pcols - LANES, pcols))
     core = slice(2 * MARGIN, prows - 2 * MARGIN)
     for way in range(2):
-        mid_out[way] = tile[:, core, ends[way]].astype(BF16)
+        mid_out[way] = packed(tile[:, core, ends[way]], way)
     for way in range(2):
         mid_copy(way).start()
 
@@ -293,7 +342,7 @@
                 ].astype(F32)
 
         for way in range(2):
-            edge_out[way, part] = tile[:, edges[part], ends[way]].astype(BF16)
+            edge_out[way, part] = packed(tile[:, edges[part], ends[way]], way)
         for way in range(2):
             edge_copy(way, part).start()
 
@@ -301,7 +350,7 @@
     inside = (row_id >= 0) & (row_id < n_dec * rows)
     deep, tall = shifts.shape[1], rows + GROUP
 
-    def match(slot, where, chosen):
+    def spread(slot, where):
         coadd[:, where] = jnp.where(
             inside, tile[0, :, where] / jnp.maximum(tile[1, :, where], 1.0), 0.0
         )
@@ -310,11 +359,9 @@
             shifts[slot, :, s * LANES : (s + 1) * LANES] = coadd[
                 first : first + deep, where
             ].astype(BF16)
-        total = None
-        for k in range(bands.shape[0]):
-            part = dot_t(shifts[slot, k * GROUP : k * GROUP + tall, :], bands[k, chosen, :])
-            total = part if total is None else total + part
-        return total
+
+    def product(slot, k, chosen):
+        return dot_t(shifts[slot, k * GROUP : k * GROUP + tall, :], bands[k, chosen, :])
 
     for part, present in ((0, has_prev), (1, has_next)):
 
@@ -323,19 +370,34 @@
             dec_core_copy(1 - part).wait_recv()
             tile[:, edges[part], LANES : 2 * LANES] += dec_core_in[1 - part].astype(F32)
 
-    inner_sum[...] = match(2, slice(LANES, 2 * LANES), slice(0, 4 * LANES))
+    spread(2, slice(LANES, 2 * LANES))
+    total = product(2, 0, slice(None))
+    for k in range(1, bands.shape[0]):
+        total = total + product(2, k, slice(None))
+    inner_sum[...] = total
 
     for way in range(2):
         mid_copy(way).wait_recv()
-        tile[:, core, ends[1 - way]] += mid_in[way].astype(F32)
+        for plane, part in enumerate(unpacked(mid_in[way], way)):
+            tile[plane, core, ends[1 - way]] += part
+    for part in range(2):
+        for way in range(2):
+            edge_copy(way, part).wait_recv()
+            for plane, value in enumerate(unpacked(edge_in[way, part], way)):
+                tile[plane, edges[part], ends[1 - way]] += value
     for end in range(2):
-        for part in range(2):
-            edge_copy(1 - end, part).wait_recv()
-            tile[:, edges[part], ends[end]] += edge_in[1 - end, part].astype(F32)
-        total = match(end, ends[end], slice((1 - end) * 2 * LANES, (2 - end) * 2 * LANES))
-        total = total + inner_sum[:, end * 2 * LANES : (end + 1) * 2 * LANES]
+        spread(end, ends[end])
+    totals = [
+        inner_sum[:, end * 2 * LANES : (end + 1) * 2 * LANES] for end in range(2)
+    ]
+    for k in range(bands.shape[0]):
+        for end in range(2):
+            totals[end] = totals[end] + product(
+                end, k, slice((1 - end) * 2 * LANES, (2 - end) * 2 * LANES)
+            )
+    for end in range(2):
         matched_ref[:, end * LANES : (end + 1) * LANES] = (
-            total[:rows, :LANES] + total[1 : rows + 1, LANES:]
+            totals[end][:rows, :LANES] + totals[end][1 : rows + 1, LANES:]
         )
     weight_ref[...] = tile[1, MARGIN : MARGIN + rows, MARGIN : MARGIN + cols]
 
@@ -396,17 +458,17 @@
                 pltpu.VMEM((2, 2, BAND, 2 * LANES), BF16),
                 pltpu.VMEM((2, 2, BAND, LANES), BF16),
                 pltpu.VMEM((2, 2, BAND, LANES), BF16),
-                pltpu.VMEM((2, 2, prows - 4 * MARGIN, LANES), BF16),
-                pltpu.VMEM((2, 2, prows - 4 * MARGIN, LANES), BF16),
-                pltpu.VMEM((2, 2, 2, BAND, LANES), BF16),
-                pltpu.VMEM((2, 2, 2, BAND, LANES), BF16),
+                pltpu.VMEM((2, (prows - 4 * MARGIN) * 3 // 2, LANES), BF16),
+                pltpu.VMEM((2, (prows - 4 * MARGIN) * 3 // 2, LANES), BF16),
+                pltpu.VMEM((2, 2, BAND * 3 // 2, LANES), BF16),
+                pltpu.VMEM((2, 2, BAND * 3 // 2, LANES), BF16),
                 pltpu.VMEM((groups * GROUP, 2 * LANES), F32),
                 pltpu.VMEM((groups, 4 * LANES, GROUP // 2 * LANES), BF16),
                 pltpu.VMEM((prows, pcols), F32),
                 pltpu.VMEM((3, deep, GROUP // 2 * LANES), BF16),
                 pltpu.VMEM((rows + GROUP, 4 * LANES), F32),
                 pltpu.SemaphoreType.DMA((4,)),
-                pltpu.SemaphoreType.DMA((3 * epochs,)),
+                pltpu.SemaphoreType.DMA((epochs, 3, 3)),
                 pltpu.SemaphoreType.DMA((2,)),
                 pltpu.SemaphoreType.DMA((2,)),
                 pltpu.SemaphoreType.DMA((2,)),

time: 17.9 us -> 17.5 us (0.978)
  Pallas kernels: 17.1 us -> 16.7 us
    pallas_call x1, Pallas kernels: 16.4 us -> 15.9 us  [shards(): pl.pallas_call(functools.partial(kernel, (epochs, prows, pcols, n_ra, n_d...]
where the time goes in v3:
time: 17.5 us; the launch traced here: 17.3 us
  Pallas kernels  16.7 us (95%)
  between operations  0.64 us (4%)
    pallas_call x1, Pallas kernels, shards(): pl.pallas_call(functools.partial(kernel, (epochs, prows, pcols, n_ra, n_d...  15.9 us
    pallas_call x1, Pallas kernels, shards(): pl.pallas_call(finish, out_shape=(result, result), in_specs=[vmem, vmem],...  0.76 us

profile of v3, /device:TPU:1, one launch (start us, length us, event | category | flops | bytes accessed | tf_op | source)
XLA Modules:
  0.0 17.3 jit_solution(15022847847420909635)
XLA Ops:
  0.6 15.9 %coadd.1 = (f32[192,256]{1,0:T(8,128)S(1)}, f32[192,256]{1,0:T(8,128)S(1)}) custom-call(f32[2,320,384]{2,1,0:T(8,128)} %exp_hbm.1, f32[2,320,384]{2,1,0:T(8,128)} %inv_hbm.1, s32[2,320,384]{2,1,0:T(8,128)} %val_hbm.1, s32[1,1,2]{2,1,0:T(1,128)} %cor_hbm.1, s32[1,1,2,2]{3,2,1,0:T(2,128)} %off_hbm.1, f32[1,1,2,2]{3,2,1,0:T(2,128)} %sub_hbm.1, ...), custom_call_target="tpu_custom_call" | custom-call | tf_op jit(solution)/shard_map/coadd/pallas_call | solution.py:442
  16.5 0.8 %finish.1 = (f32[192,256]{1,0:T(8,128)}, f32[192,256]{1,0:T(8,128)}) custom-call(f32[192,256]{1,0:T(8,128)S(1)} %get-tuple-element.4.matched_in, f32[192,256]{1,0:T(8,128)S(1)} %get-tuple-element.5.weight_in), custom_call_target="tpu_custom_call" | custom-call | tf_op jit(solution)/shard_map/finish/pallas_call | solution.py:486

commit v4 on v3

--- a/solution.py
+++ b/solution.py
@@ -346,19 +346,17 @@
         for way in range(2):
             edge_copy(way, part).start()
 
-    row_id = lax.broadcasted_iota(jnp.int32, (prows, 1), 0) - MARGIN + me_dec * rows
+    span = coadd.shape[0]
+    row_id = lax.broadcasted_iota(jnp.int32, (span, 1), 0) - HALF + me_dec * rows
     inside = (row_id >= 0) & (row_id < n_dec * rows)
     deep, tall = shifts.shape[1], rows + GROUP
 
     def spread(slot, where):
-        coadd[:, where] = jnp.where(
-            inside, tile[0, :, where] / jnp.maximum(tile[1, :, where], 1.0), 0.0
-        )
+        numer = tile[0, offset : offset + span, where]
+        denom = tile[1, offset : offset + span, where]
+        coadd[:, where] = jnp.where(inside, numer / jnp.maximum(denom, 1.0), 0.0).astype(BF16)
         for s in range(GROUP // 2):
-            first = offset + 2 * s
-            shifts[slot, :, s * LANES : (s + 1) * LANES] = coadd[
-                first : first + deep, where
-            ].astype(BF16)
+            shifts[slot, :, s * LANES : (s + 1) * LANES] = coadd[2 * s : 2 * s + deep, where]
 
     def product(slot, k, chosen):
         return dot_t(shifts[slot, k * GROUP : k * GROUP + tall, :], bands[k, chosen, :])
@@ -464,7 +462,7 @@
                 pltpu.VMEM((2, 2, BAND * 3 // 2, LANES), BF16),
                 pltpu.VMEM((groups * GROUP, 2 * LANES), F32),
                 pltpu.VMEM((groups, 4 * LANES, GROUP // 2 * LANES), BF16),
-                pltpu.VMEM((prows, pcols), F32),
+                pltpu.VMEM((deep + GROUP, pcols), BF16),
                 pltpu.VMEM((3, deep, GROUP // 2 * LANES), BF16),
                 pltpu.VMEM((rows + GROUP, 4 * LANES), F32),
                 pltpu.SemaphoreType.DMA((4,)),

time: 17.5 us -> 17.3 us (0.989)
  Pallas kernels: 16.7 us -> 16.4 us
    pallas_call x1, Pallas kernels: 15.9 us -> 15.7 us  [shards(): pl.pallas_call(functools.partial(kernel, (epochs, prows, pcols, n_ra, n_d...]
where the time goes in v4:
time: 17.3 us; the launch traced here: 17.1 us
  Pallas kernels  16.4 us (95%)
  between operations  0.64 us (4%)
    pallas_call x1, Pallas kernels, shards(): pl.pallas_call(functools.partial(kernel, (epochs, prows, pcols, n_ra, n_d...  15.7 us
    pallas_call x1, Pallas kernels, shards(): pl.pallas_call(finish, out_shape=(result, result), in_specs=[vmem, vmem],...  0.76 us

profile of v4, /device:TPU:1, one launch (start us, length us, event | category | flops | bytes accessed | tf_op | source)
XLA Modules:
  0.0 17.1 jit_solution(8976603338921517121)
XLA Ops:
  0.6 15.7 %coadd.1 = (f32[192,256]{1,0:T(8,128)S(1)}, f32[192,256]{1,0:T(8,128)S(1)}) custom-call(f32[2,320,384]{2,1,0:T(8,128)} %exp_hbm.1, f32[2,320,384]{2,1,0:T(8,128)} %inv_hbm.1, s32[2,320,384]{2,1,0:T(8,128)} %val_hbm.1, s32[1,1,2]{2,1,0:T(1,128)} %cor_hbm.1, s32[1,1,2,2]{3,2,1,0:T(2,128)} %off_hbm.1, f32[1,1,2,2]{3,2,1,0:T(2,128)} %sub_hbm.1, ...), custom_call_target="tpu_custom_call" | custom-call | tf_op jit(solution)/shard_map/coadd/pallas_call | solution.py:440
  16.3 0.8 %finish.1 = (f32[192,256]{1,0:T(8,128)}, f32[192,256]{1,0:T(8,128)}) custom-call(f32[192,256]{1,0:T(8,128)S(1)} %get-tuple-element.4.matched_in, f32[192,256]{1,0:T(8,128)S(1)} %get-tuple-element.5.weight_in), custom_call_target="tpu_custom_call" | custom-call | tf_op jit(solution)/shard_map/finish/pallas_call | solution.py:484
